TPU v7x, 32 devices: a whole 2x2x4 slice. The times are simulated.
32 devices in a mesh: fsdp: 16 (over z, y, core), sp: 2 (over x).
Axes of the slice: x: 2, y: 2, z: 4, core: 2. Of those that a mesh axis runs over, the one named last changes fastest.
Arguments:
- latents: bfloat16 [32, 256, 768], P('fsdp', 'sp'), may hold values from -6 to 6
- condition: bfloat16 [32, 768], P('fsdp'), may hold values from -6 to 6
- cotangent: bfloat16 [32, 256, 768], P('fsdp', 'sp'), may hold values from -6 to 6
- w_ada: bfloat16 [768, 4608], P('fsdp'), may hold values from -0.21875 to 0.21875
- b_ada: bfloat16 [4608], P('fsdp'), may hold values from -3 to 3
- w_qkv: bfloat16 [768, 2304], P('fsdp'), may hold values from -0.21875 to 0.21875
- b_query: bfloat16 [768], P('fsdp'), may hold values from -3 to 3
- b_value: bfloat16 [768], P('fsdp'), may hold values from -3 to 3
- w_out: bfloat16 [768, 768], P('fsdp'), may hold values from -0.875 to 0.875
- b_out: bfloat16 [768], P('fsdp'), may hold values from -3 to 3
- w_up: bfloat16 [768, 3072], P('fsdp'), may hold values from -0.21875 to 0.21875
- b_up: bfloat16 [3072], P('fsdp'), may hold values from -3 to 3
- w_down: bfloat16 [3072, 768], P('fsdp'), may hold values from -0.109375 to 0.109375
- b_down: bfloat16 [768], P('fsdp'), may hold values from -3 to 3
Outputs:
- output: bfloat16 [32, 256, 768], P('fsdp', 'sp')
- grad_latents: float32 [32, 256, 768], P('fsdp', 'sp')
- grad_condition: float32 [32, 768], P('fsdp')
- grad_w_ada: float32 [768, 4608], P(('fsdp', 'sp'))
- grad_b_ada: float32 [4608], P(('fsdp', 'sp'))
- grad_w_qkv: float32 [768, 2304], P(('fsdp', 'sp'))
- grad_b_query: float32 [768], P(('fsdp', 'sp'))
- grad_b_value: float32 [768], P(('fsdp', 'sp'))
- grad_w_out: float32 [768, 768], P(('fsdp', 'sp'))
- grad_b_out: float32 [768], P(('fsdp', 'sp'))
- grad_w_up: float32 [768, 3072], P(('fsdp', 'sp'))
- grad_b_up: float32 [3072], P(('fsdp', 'sp'))
- grad_w_down: float32 [3072, 768], P(('fsdp', 'sp'))
- grad_b_down: float32 [768], P(('fsdp', 'sp'))
All inputs are finite; a program needn't handle non-finite values.
Results may differ from a plain program's by a relative error of at most 0.015.
The roundings to bfloat16 on the way count: a program that leaves them out, or rounds other values in their place, can miss the bound.
Values may be sent and summed in bfloat16 or wider, within the bound.
A program may use at most 256 MiB of HBM per device.

v0:
```python
import jax
import jax.numpy as jnp
from jax import lax
from jax.sharding import PartitionSpec as P

D = 768
H = 12
HD = 64


eps = 1e-06


def normalize(values):
    centered = values - jnp.mean(values, axis=-1, keepdims=True)
    inverse = lax.rsqrt(jnp.mean(centered * centered, axis=-1, keepdims=True) + eps)
    return (centered * inverse, inverse)


def norm_back(grad_in, normed, inverse):
    return inverse * (
        grad_in
        - jnp.mean(grad_in, axis=-1, keepdims=True)
        - normed * jnp.mean(grad_in * normed, axis=-1, keepdims=True)
    )


def gelu_tanh(values):
    return jax.nn.gelu(values, approximate=True)


def silu_back(values, grad_out):
    return jax.vjp(jax.nn.silu, values)[1](grad_out)[0]


def gelu_back(values, grad_out):
    return jax.vjp(gelu_tanh, values)[1](grad_out)[0]


def micro_pass(latents, condition, cotangent, shards):
    f32 = jnp.float32
    bf16 = jnp.bfloat16
    batch_count = latents.shape[0]
    half_tokens = latents.shape[1]
    groups = lax.axis_size("sp")
    tokens_all = half_tokens * groups
    heads_local = H // groups
    scale_factor = HD ** (-0.5)
    full_fwd = (
        lax.all_gather(shards[0], "fsdp", axis=0, tiled=True),
        lax.all_gather(shards[1], "fsdp", axis=0, tiled=True),
        lax.all_gather(shards[2], "fsdp", axis=0, tiled=True),
        lax.all_gather(shards[3], "fsdp", axis=0, tiled=True),
        lax.all_gather(shards[4], "fsdp", axis=0, tiled=True),
        lax.all_gather(shards[5], "fsdp", axis=0, tiled=True),
        lax.all_gather(shards[6], "fsdp", axis=0, tiled=True),
        lax.all_gather(shards[7], "fsdp", axis=0, tiled=True),
        lax.all_gather(shards[8], "fsdp", axis=0, tiled=True),
        lax.all_gather(shards[9], "fsdp", axis=0, tiled=True),
        lax.all_gather(shards[10], "fsdp", axis=0, tiled=True),
    )
    (
        ada_full,
        ada_bias,
        qkv_full,
        query_bias,
        value_bias,
        out_full,
        out_bias,
        up_full,
        up_bias,
        down_full,
        down_bias,
    ) = full_fwd
    cond_float = condition.astype(f32)
    silu_cond = jax.nn.silu(cond_float)
    modulate = jnp.dot(
        silu_cond.astype(bf16), ada_full, preferred_element_type=f32
    ) + ada_bias.astype(f32)
    mod_parts = modulate.reshape(batch_count, 6, 1, D)
    shift_one, scale_one, gate_one = (mod_parts[:, 0], mod_parts[:, 1], mod_parts[:, 2])
    shift_two, scale_two, gate_two = (mod_parts[:, 3], mod_parts[:, 4], mod_parts[:, 5])
    inputs = latents.astype(f32)
    normed_one, inverse_one = normalize(inputs)
    attn_in = (normed_one * (1.0 + scale_one) + shift_one).astype(bf16)
    qkv_bias = jnp.concatenate([query_bias, jnp.zeros_like(query_bias), value_bias]).astype(f32)
    projected = (
        jnp.einsum("btd,de->bte", attn_in, qkv_full, preferred_element_type=f32) + qkv_bias
    ).astype(bf16)
    projected = projected.reshape(batch_count, half_tokens, 3, groups, heads_local * HD)
    head_layout = lax.all_to_all(projected, "sp", split_axis=3, concat_axis=1, tiled=True)
    queries = head_layout[:, :, 0, 0].reshape(batch_count, tokens_all, heads_local, HD)
    key_heads = head_layout[:, :, 1, 0].reshape(batch_count, tokens_all, heads_local, HD)
    value_heads = head_layout[:, :, 2, 0].reshape(batch_count, tokens_all, heads_local, HD)
    scores = (
        jnp.einsum("bqhd,bkhd->bhqk", queries, key_heads, preferred_element_type=f32) * scale_factor
    )
    log_total = jnp.log(jnp.sum(jnp.exp(scores), axis=-1, keepdims=True))
    soft_half = jnp.exp(scores - log_total).astype(bf16)
    mixed = jnp.einsum(
        "bhqk,bkhd->bqhd", soft_half, value_heads, preferred_element_type=f32
    ).astype(bf16)
    mixed = mixed.reshape(batch_count, tokens_all, 1, heads_local * HD)
    mixed_tokens = lax.all_to_all(mixed, "sp", split_axis=1, concat_axis=2, tiled=True).reshape(
        batch_count, half_tokens, D
    )
    attn_proj = jnp.einsum(
        "btd,de->bte", mixed_tokens, out_full, preferred_element_type=f32
    ) + out_bias.astype(f32)
    residual = inputs + gate_one * attn_proj
    normed_two, inverse_two = normalize(residual)
    mlp_in = (normed_two * (1.0 + scale_two) + shift_two).astype(bf16)
    up_value = jnp.einsum(
        "btd,df->btf", mlp_in, up_full, preferred_element_type=f32
    ) + up_bias.astype(f32)
    activated = gelu_tanh(up_value).astype(bf16)
    down_value = jnp.einsum(
        "btf,fd->btd", activated, down_full, preferred_element_type=f32
    ) + down_bias.astype(f32)
    output = (residual + gate_two * down_value).astype(bf16)
    full_bwd = (
        lax.all_gather(shards[0], "fsdp", axis=0, tiled=True),
        lax.all_gather(shards[1], "fsdp", axis=0, tiled=True),
        lax.all_gather(shards[2], "fsdp", axis=0, tiled=True),
        lax.all_gather(shards[3], "fsdp", axis=0, tiled=True),
        lax.all_gather(shards[4], "fsdp", axis=0, tiled=True),
        lax.all_gather(shards[5], "fsdp", axis=0, tiled=True),
        lax.all_gather(shards[6], "fsdp", axis=0, tiled=True),
        lax.all_gather(shards[7], "fsdp", axis=0, tiled=True),
        lax.all_gather(shards[8], "fsdp", axis=0, tiled=True),
        lax.all_gather(shards[9], "fsdp", axis=0, tiled=True),
        lax.all_gather(shards[10], "fsdp", axis=0, tiled=True),
    )
    ada_back = full_bwd[0]
    qkv_back = full_bwd[2]
    out_back = full_bwd[5]
    up_back = full_bwd[7]
    down_back = full_bwd[9]
    grad_out = cotangent.astype(f32)
    grad_gate_two = jnp.sum(grad_out * down_value, axis=1)
    grad_down = (grad_out * gate_two).astype(bf16)
    gw_down = jnp.einsum("btf,btd->fd", activated, grad_down, preferred_element_type=f32)
    gb_down = jnp.sum(grad_down.astype(f32), axis=(0, 1))
    grad_act = jnp.einsum("btd,fd->btf", grad_down, down_back, preferred_element_type=f32)
    grad_up = gelu_back(up_value, grad_act).astype(bf16)
    gw_up = jnp.einsum("btd,btf->df", mlp_in, grad_up, preferred_element_type=f32)
    gb_up = jnp.sum(grad_up.astype(f32), axis=(0, 1))
    grad_mlp = jnp.einsum("btf,df->btd", grad_up, up_back, preferred_element_type=f32)
    grad_scale_two = jnp.sum(grad_mlp * normed_two, axis=1)
    grad_shift_two = jnp.sum(grad_mlp, axis=1)
    grad_resid = grad_out + norm_back(grad_mlp * (1.0 + scale_two), normed_two, inverse_two)
    grad_gate_one = jnp.sum(grad_resid * attn_proj, axis=1)
    grad_proj = (grad_resid * gate_one).astype(bf16)
    gw_out = jnp.einsum("btd,bte->de", mixed_tokens, grad_proj, preferred_element_type=f32)
    gb_out = jnp.sum(grad_proj.astype(f32), axis=(0, 1))
    grad_mixed = jnp.einsum("bte,de->btd", grad_proj, out_back, preferred_element_type=f32).astype(
        bf16
    )
    grad_mixed = grad_mixed.reshape(batch_count, half_tokens, groups, heads_local * HD)
    grad_heads = lax.all_to_all(grad_mixed, "sp", split_axis=2, concat_axis=1, tiled=True).reshape(
        batch_count, tokens_all, heads_local, HD
    )
    scores_again = (
        jnp.einsum("bqhd,bkhd->bhqk", queries, key_heads, preferred_element_type=f32) * scale_factor
    )
    soft_float = jnp.exp(scores_again - log_total)
    soft_again = soft_float.astype(bf16)
    grad_soft = jnp.einsum("bqhd,bkhd->bhqk", grad_heads, value_heads, preferred_element_type=f32)
    delta_sum = jnp.sum(soft_float * grad_soft, axis=-1, keepdims=True)
    grad_scores = (soft_float * (grad_soft - delta_sum)).astype(bf16)
    grad_queries = (
        jnp.einsum("bhqk,bkhd->bqhd", grad_scores, key_heads, preferred_element_type=f32)
        * scale_factor
    ).astype(bf16)
    grad_keys = (
        jnp.einsum("bhqk,bqhd->bkhd", grad_scores, queries, preferred_element_type=f32)
        * scale_factor
    ).astype(bf16)
    grad_values = jnp.einsum(
        "bhqk,bqhd->bkhd", soft_again, grad_heads, preferred_element_type=f32
    ).astype(bf16)
    grad_stack = jnp.stack([grad_queries, grad_keys, grad_values], axis=2).reshape(
        batch_count, tokens_all, 3, 1, heads_local * HD
    )
    grad_tokens = lax.all_to_all(grad_stack, "sp", split_axis=1, concat_axis=3, tiled=True).reshape(
        batch_count, half_tokens, 3 * D
    )
    gw_qkv = jnp.einsum("btd,bte->de", attn_in, grad_tokens, preferred_element_type=f32)
    grad_tok_float = grad_tokens.astype(f32)
    gb_query = jnp.sum(grad_tok_float[:, :, :D], axis=(0, 1))
    gb_value = jnp.sum(grad_tok_float[:, :, 2 * D :], axis=(0, 1))
    grad_attn_in = jnp.einsum("bte,de->btd", grad_tokens, qkv_back, preferred_element_type=f32)
    grad_scale_one = jnp.sum(grad_attn_in * normed_one, axis=1)
    grad_shift_one = jnp.sum(grad_attn_in, axis=1)
    grad_latents = grad_resid + norm_back(grad_attn_in * (1.0 + scale_one), normed_one, inverse_one)
    grad_mod_part = jnp.concatenate(
        [
            grad_shift_one,
            grad_scale_one,
            grad_gate_one,
            grad_shift_two,
            grad_scale_two,
            grad_gate_two,
        ],
        axis=1,
    )
    gw_ada = jnp.dot(silu_cond.T, grad_mod_part, precision=lax.Precision.HIGHEST)
    gb_ada = jnp.sum(grad_mod_part, axis=0)
    grad_mod_total = lax.psum(grad_mod_part, "sp")
    grad_silu = jnp.dot(grad_mod_total.astype(bf16), ada_back.T, preferred_element_type=f32)
    grad_condition = silu_back(cond_float, grad_silu)
    grads = (
        gw_ada,
        gb_ada,
        gw_qkv,
        gb_query,
        gb_value,
        gw_out,
        gb_out,
        gw_up,
        gb_up,
        gw_down,
        gb_down,
    )
    return (output, grad_latents, grad_condition, grads)


def body(
    latents,
    condition,
    cotangent,
    w_ada,
    b_ada,
    w_qkv,
    b_query,
    b_value,
    w_out,
    b_out,
    w_up,
    b_up,
    w_down,
    b_down,
):
    shards = (w_ada, b_ada, w_qkv, b_query, b_value, w_out, b_out, w_up, b_up, w_down, b_down)
    outputs = []
    grad_inputs = []
    grad_conds = []
    running = None
    for micro in range(latents.shape[0]):
        output, grad_latents, grad_condition, grads = micro_pass(
            latents[micro : micro + 1],
            condition[micro : micro + 1],
            cotangent[micro : micro + 1],
            shards,
        )
        outputs.append(output)
        grad_inputs.append(grad_latents)
        grad_conds.append(grad_condition)
        running = grads if running is None else jax.tree.map(jnp.add, running, grads)
    fsdp_count = lax.axis_size("fsdp")
    sp_count = lax.axis_size("sp")
    owners = fsdp_count * sp_count
    packed = jnp.concatenate([grad.reshape(owners, -1) for grad in running], axis=1)
    owned_flat = lax.psum_scatter(packed, ("fsdp", "sp"), scatter_dimension=0, tiled=True).reshape(
        -1
    )
    owned = []
    start = 0
    for grad in running:
        width = grad.size // owners
        piece = owned_flat[start : start + width]
        owned.append(piece.reshape((grad.shape[0] // owners,) + grad.shape[1:]))
        start = start + width
    return (
        jnp.concatenate(outputs, axis=0),
        jnp.concatenate(grad_inputs, axis=0),
        jnp.concatenate(grad_conds, axis=0),
        owned[0],
        owned[1],
        owned[2],
        owned[3],
        owned[4],
        owned[5],
        owned[6],
        owned[7],
        owned[8],
        owned[9],
        owned[10],
    )


def solution(mesh):
    in_specs = (
        P("fsdp", "sp", None),
        P("fsdp", None),
        P("fsdp", "sp", None),
        P("fsdp", None),
        P("fsdp"),
        P("fsdp", None),
        P("fsdp"),
        P("fsdp"),
        P("fsdp", None),
        P("fsdp"),
        P("fsdp", None),
        P("fsdp"),
        P("fsdp", None),
        P("fsdp"),
    )
    out_specs = (
        P("fsdp", "sp", None),
        P("fsdp", "sp", None),
        P("fsdp", None),
        P(("fsdp", "sp"), None),
        P(("fsdp", "sp")),
        P(("fsdp", "sp"), None),
        P(("fsdp", "sp")),
        P(("fsdp", "sp")),
        P(("fsdp", "sp"), None),
        P(("fsdp", "sp")),
        P(("fsdp", "sp"), None),
        P(("fsdp", "sp")),
        P(("fsdp", "sp"), None),
        P(("fsdp", "sp")),
    )
    return jax.shard_map(body, mesh=mesh, in_specs=in_specs, out_specs=out_specs, check_vma=False)
```

profile of v0, /device:TPU:0, one launch (start us, length us, event | category | flops | bytes accessed | tf_op | source)
XLA Modules:
  0.0 1298.5 jit_solution(7892123510075763174)
XLA Ops:
  18.9 65.8 %all-reduce.8 = (bf16[768]{0:T(1024)(128)(2,1)S(1)}, bf16[768]{0:T(1024)(128)(2,1)S(1)}, bf16[4608]{0:T(1024)(128)(2,1)S(1)}, bf16[3072]{0:T(1024)(128)(2,1)S(1)...) all-reduce(bf16[768]{0:T(1024)(128)(2,1)S(1)} %dynamic-update-slice, ...), channel_id=1, replica_groups=mesh['fsdp'=16,'sp'=2] {'fsdp'}, use_global_device_ids=true, to_apply=%add.2 | all-reduce | flops 10752 | bytes 43008
  85.7 4.3 convolution_reduce_fusion.1
  92.1 36.1 %all-gather.8.cloned.1.call-done = bf16[768,2304]{1,0:T(8,128)(2,1)} async-done(((bf16[48,2304]{1,0:T(8,128)(2,1)}), bf16[768,2304]{1,0:T(8,128)(2,1)}) %all-gather.8.cloned.1.call-update) | async-done | bytes 3538960 | tf_op jit(solution)/shard_map/all_gather | solution.py:52
  132.0 3.5 all-to-all-start
  136.6 8.2 all-to-all-done
  150.0 4.0 all-to-all-start.1
  154.6 4.2 all-to-all-done.1
  159.2 8.2 all-gather.10.cloned.1.call-done
  170.0 51.6 %all-gather.12.cloned.1.call-done = bf16[768,3072]{1,0:T(8,128)(2,1)} async-done(((bf16[48,3072]{1,0:T(8,128)(2,1)}), bf16[768,3072]{1,0:T(8,128)(2,1)}) %all-gather.12.cloned.1.call-update) | async-done | bytes 4718608 | tf_op jit(solution)/shard_map/all_gather | solution.py:57
  224.9 50.5 %all-gather.14.cloned.1.call-done = bf16[3072,768]{1,0:T(8,128)(2,1)} async-done(((bf16[192,768]{1,0:T(8,128)(2,1)}), bf16[3072,768]{1,0:T(8,128)(2,1)}) %all-gather.14.cloned.1.call-update) | async-done | bytes 4718608 | tf_op jit(solution)/shard_map/all_gather | solution.py:59
  275.4 5.1 convert_reduce_fusion.1
  287.9 3.4 all-to-all-start.4
  291.4 6.2 fusion.106
  308.7 3.7 all-to-all-start.5
  312.5 5.2 fusion.151
  319.5 4.4 all-to-all-done.5
  326.3 5.6 fusion.146
  341.9 4.2 all-to-all-start.2
  349.9 4.9 all-to-all-done.2
  369.7 3.4 reduce.107
  374.8 4.3 all-to-all-start.3
  379.7 4.3 all-to-all-done.3
  389.2 3.7 fusion.65
  393.2 3.3 convolution_add_fusion.5
  396.6 6.1 convert_reduce_fusion
  415.1 4.3 all-to-all-start.6
  419.4 3.7 convolution_add_fusion.7
  428.6 9.3 convolution_add_fusion.2
  437.9 8.2 reshape.826
  448.8 9.6 convolution_add_fusion.1
  458.4 8.0 reshape.827
  486.7 3.5 pad_maximum_fusion.1
  490.1 4.3 all-to-all-start.7
  497.4 5.8 all-to-all-done.7
  513.3 7.2 multiply_add_fusion
  520.5 10.7 reshape.823
  531.2 10.9 constant_dynamic-update-slice_fusion.12
  542.3 7.3 convolution_add_fusion
  549.5 6.7 reshape.824
  558.2 20.7 %dynamic-update-slice.8 = f32[32,332112]{1,0:T(8,128)} dynamic-update-slice(f32[32,332112]{1,0:T(8,128)} %dynamic-update-slice.7, f32[32,55296]{1,0:T(8,128)} %reshape.824, s32[]{} %constant.118, s32[]{} %constant.120) | dynamic-update-slice | bytes 14155780
  581.8 8.9 dynamic-update-slice.11
  592.3 28.8 %dynamic-update-slice.13 = f32[32,332112]{1,0:T(8,128)} dynamic-update-slice(f32[32,332112]{1,0:T(8,128)} %dynamic-update-slice.12, f32[32,73728]{1,0:T(8,128)} %reshape.826, s32[]{} %constant.118, s32[]{} %constant.125) | dynamic-update-slice | bytes 18874372
  622.6 28.3 %dynamic-update-slice.15 = f32[32,332112]{1,0:T(8,128)} dynamic-update-slice(f32[32,332112]{1,0:T(8,128)} %dynamic-update-slice.14, f32[32,73728]{1,0:T(8,128)} %reshape.827, s32[]{} %constant.118, s32[]{} %constant.127) | dynamic-update-slice | bytes 18874372
  654.1 18.4 %all-reduce.7 = (bf16[1,4608]{1,0:T(2,128)(2,1)S(1)}, bf16[1,4608]{1,0:T(2,128)(2,1)S(1)}) all-reduce(f32[1,4608]{1,0:T(1,128)S(1)} %constant_dynamic-update-slice_fusion.6, f32[1,4608]{1,0:T(1,128)S(1)} %copy-done.45), channel_id=1, replica_groups=mesh['fsdp'=16,'sp'=2] {'sp'}, use_global_device_ids=true, to_apply=%region_33.34 | all-reduce | flops 9216 | bytes 55296 | tf_op jit(solution)/shard_map/psum | solution.py:209
  672.5 5.1 fusion.125
  677.6 5.1 fusion.123
  684.3 588.6 %all-reduce.11.cloned.1.call-done = f32[32,332112]{1,0:T(8,128)} async-done(((f32[32,332112]{1,0:T(8,128)}), f32[32,332112]{1,0:T(8,128)}) %all-reduce.11.cloned.1.call-update) | async-done | bytes 42510352
  1281.8 4.1 dynamic-slice_reduce_fusion.1
  (373 shorter events, 169.4 us)
Async XLA Ops:
  7.2 78.1 %copy-start.6 = (bf16[2,128,768]{2,1,0:T(8,128)(2,1)S(1)}, bf16[2,128,768]{2,1,0:T(8,128)(2,1)}, u32[]{:S(2)}) copy-start(bf16[2,128,768]{2,1,0:T(8,128)(2,1)} %param.14) | copy-start | bytes 1179652
  7.2 78.5 %copy-start.41 = (bf16[2,768]{1,0:T(2,128)(2,1)S(1)}, bf16[2,768]{1,0:T(2,128)(2,1)}, u32[]{:S(2)}) copy-start(bf16[2,768]{1,0:T(2,128)(2,1)} %param.15) | copy-start | bytes 9220
  7.2 78.5 %all-gather.6.cloned.1.call-start = ((), (), s32[]{:S(2)}) async-start(), calls=%async_computation.8 | async-start | bytes 7520256 | tf_op jit(solution)/shard_map/all_gather | solution.py:50
  7.9 120.3 %all-gather.8.cloned.1.call-start = ((), (), s32[]{:S(2)}) async-start(), calls=%async_computation.9 | async-start | bytes 3760128 | tf_op jit(solution)/shard_map/all_gather | solution.py:52
  8.7 158.7 %all-gather.10.cloned.1.call-start = ((), (), s32[]{:S(2)}) async-start(), calls=%async_computation.10 | async-start | bytes 1253376 | tf_op jit(solution)/shard_map/all_gather | solution.py:55
  9.4 212.1 %all-gather.12.cloned.1.call-start = ((), (), s32[]{:S(2)}) async-start(), calls=%async_computation.11 | async-start | bytes 5013504 | tf_op jit(solution)/shard_map/all_gather | solution.py:57
  10.0 265.4 %all-gather.14.cloned.1.call-start = ((), (), s32[]{:S(2)}) async-start(), calls=%async_computation.12 | async-start | bytes 5013504 | tf_op jit(solution)/shard_map/all_gather | solution.py:59
  85.3 136.3 %copy-start.39 = (f32[3072]{0:T(1024)}, f32[3072]{0:T(1024)S(1)}, u32[]{:S(2)}) copy-start(f32[3072]{0:T(1024)S(1)} %convert_element_type.267) | copy-start | bytes 36868
  85.3 82.1 %copy-start.51 = (f32[768]{0:T(1024)}, f32[768]{0:T(1024)S(1)}, u32[]{:S(2)}) copy-start(f32[768]{0:T(1024)S(1)} %convert_element_type.265) | copy-start | bytes 9220
  85.3 42.9 %copy-start.42 = (f32[2304]{0:T(1024)}, f32[2304]{0:T(1024)S(1)}, u32[]{:S(2)}) copy-start(f32[2304]{0:T(1024)S(1)} %maximum_convert_fusion) | copy-start | bytes 27652
  85.5 42.8 %copy-start.69 = (f32[128]{0:T(128)}, f32[128]{0:T(128)S(1)}, u32[]{:S(2)}) copy-start(f32[128]{0:T(128)S(1)} %broadcast_multiply_fusion.11) | copy-start | bytes 1540
  85.7 42.6 %copy-start.79 = (f32[128]{0:T(128)}, f32[128]{0:T(128)S(1)}, u32[]{:S(2)}) copy-start(f32[128]{0:T(128)S(1)} %add_rsqrt_fusion.3) | copy-start | bytes 1540
  92.1 199.2 %copy-start.59 = (f32[768]{0:T(1024)}, f32[768]{0:T(1024)S(1)}, u32[]{:S(2)}) copy-start(f32[768]{0:T(1024)S(1)} %get-tuple-element.46) | copy-start | bytes 9220
  132.0 12.8 all-to-all-start
  150.0 8.8 all-to-all-start.1
  159.2 62.4 %copy-start.26 = (bf16[1,128,2,1,384]{1,4,2,3,0:T(8,128)(2,1)}, bf16[1,128,2,1,384]{1,4,2,3,0:T(8,128)(2,1)S(1)}, u32[]{:S(2)}) copy-start(bf16[1,128,2,1,384]{1,4,2,3,0:T(8,128)(2,1)S(1)} %copy.95) | copy-start | bytes 589828
  169.8 142.7 %copy-start.4 = (f32[1,128,768]{2,1,0:T(8,128)}, f32[1,128,768]{2,1,0:T(8,128)S(1)}, u32[]{:S(2)}) copy-start(f32[1,128,768]{2,1,0:T(8,128)S(1)} %get-tuple-element.77) | copy-start | bytes 1179652
  221.6 59.0 %slice-start = ((s8[4718592]{0:T(1024)(128)(4,1)}), s8[524288]{0:T(1024)(128)(4,1)S(1)}, s32[]{:S(2)}) async-start(s8[4718592]{0:T(1024)(128)(4,1)} %bitcast.282), calls=%async_computation.14 | async-start | bytes 1048576
  224.8 66.5 %copy-start.12 = (f32[128,3072]{1,0:T(8,128)}, f32[128,3072]{1,0:T(8,128)S(1)}, u32[]{:S(2)}) copy-start(f32[128,3072]{1,0:T(8,128)S(1)} %convolution_add_fusion.6) | copy-start | bytes 4718596
  287.9 9.6 all-to-all-start.4
  308.7 15.2 %all-to-all-start.5 = ((bf16[1,256,3,1,384]{4,2,3,0,1:T(4,128)(2,1)}), bf16[1,256,3,1,384]{4,2,3,0,1:T(4,128)(2,1)S(1)}, u32[]{:S(2)}, u32[]{:S(2)}) async-start(bf16[1,256,3,1,384]{4,2,3,0,1:T(4,128)(2,1)} %pad_maximum_fusion), calls=%async_computation.5 | async-start | bytes 1572864 | tf_op jit(solution)/shard_map/all_to_all | solution.py:185
  340.0 8.2 copy-start.58
  341.9 12.9 all-to-all-start.2
  364.6 14.5 %copy-start.83 = (f32[768]{0:T(1024)S(1)}, f32[768]{0:T(1024)}, u32[]{:S(2)}) copy-start(f32[768]{0:T(1024)} %get-tuple-element.22) | copy-start | bytes 9220
  374.8 9.2 all-to-all-start.3
  392.9 13.9 %copy-start.10 = (f32[1,128,768]{2,1,0:T(8,128)}, f32[1,128,768]{2,1,0:T(8,128)S(1)}, u32[]{:S(2)}) copy-start(f32[1,128,768]{2,1,0:T(8,128)S(1)} %get-tuple-element.96) | copy-start | bytes 1179652
  392.9 13.9 %copy-start.71 = (f32[128]{0:T(128)}, f32[128]{0:T(128)S(1)}, u32[]{:S(2)}) copy-start(f32[128]{0:T(128)S(1)} %broadcast_multiply_fusion.8) | copy-start | bytes 1540
  393.1 13.7 %copy-start.81 = (f32[128]{0:T(128)}, f32[128]{0:T(128)S(1)}, u32[]{:S(2)}) copy-start(f32[128]{0:T(128)S(1)} %add_rsqrt_fusion) | copy-start | bytes 1540
  393.2 9.5 slice-start.2
  393.2 12.4 slice-start.4
  396.5 9.1 copy-start.14
  396.6 9.0 slice-start.5
  415.1 53.3 %all-to-all-start.6 = ((bf16[1,128,2,384]{3,1,0,2:T(8,128)(2,1)}), bf16[1,128,2,384]{3,1,0,2:T(8,128)(2,1)}, u32[]{:S(2)}, u32[]{:S(2)}) async-start(bf16[1,128,2,384]{3,1,0,2:T(8,128)(2,1)} %copy.114), calls=%async_computation.6 | async-start | bytes 393216 | tf_op jit(solution)/shard_map/all_to_all | solution.py:160
  437.9 10.9 copy-start.68
  458.4 9.4 copy-start.63
  486.7 8.3 copy-start.56
  486.7 8.9 copy-start.61
  490.1 13.0 %all-to-all-start.7 = ((bf16[1,256,3,1,384]{4,2,3,0,1:T(4,128)(2,1)}), bf16[1,256,3,1,384]{4,2,3,0,1:T(4,128)(2,1)}, u32[]{:S(2)}, u32[]{:S(2)}) async-start(bf16[1,256,3,1,384]{4,2,3,0,1:T(4,128)(2,1)} %pad_maximum_fusion.1), calls=%async_computation.7 | async-start | bytes 1572864 | tf_op jit(solution)/shard_map/all_to_all | solution.py:185
  494.4 778.5 %all-reduce.11.cloned.1.call-start = ((), (), s32[]{:S(2)}) async-start(), calls=%async_computation.13 | async-start | bytes 85032960
  531.2 11.1 copy-start.9
  531.2 11.1 copy-start.18
  531.2 11.1 copy-start.53
  531.2 11.1 copy-start.75
  531.2 11.1 copy-start.78
  558.2 23.7 %copy-start.11 = (f32[32,18432]{1,0:T(8,128)S(1)}, f32[32,18432]{1,0:T(8,128)}, u32[]{:S(2)}) copy-start(f32[32,18432]{1,0:T(8,128)} %reshape.825) | copy-start | bytes 7077892
  581.8 8.9 copy-start.46
  592.3 28.8 %copy-start.47 = (f32[32,96]{1,0:T(8,128)S(1)}, f32[32,96]{1,0:T(8,128)}, u32[]{:S(2)}) copy-start(f32[32,96]{1,0:T(8,128)} %add.388) | copy-start | bytes 36868
  622.6 28.3 %copy-start.48 = (f32[32,24]{1,0:T(8,128)S(1)}, f32[32,24]{1,0:T(8,128)}, u32[]{:S(2)}) copy-start(f32[32,24]{1,0:T(8,128)} %add.391) | copy-start | bytes 9220
  (57 other events, 178.4 us)
Sparse Core Ops, SparseCore 0:
  10.3 69.7 all-gather.5
  82.4 45.8 all-gather.7
  130.5 36.8 all-gather.9
  169.5 51.9 all-gather.11
  223.7 51.6 all-gather.13
  652.5 620.3 all-reduce.10
where the time goes:
time: 1310 us; the launch traced here: 1300 us
  waiting for transfers between devices  770 us (59%)
  local copies, waits for them, and re-layouts  231 us (18%)
  matrix products  126 us (10%)
  blocking collectives  84.2 us (6%)
  other arithmetic  38 us (3%)
  starting transfers between devices  32.4 us (2%)
  between operations  17.5 us (1%)
    unnamed x7, waiting for transfers between devices  592 us
    unnamed x223, local copies, waits for them, and re-layouts  126 us
    unnamed x1, blocking collectives  65.8 us
    all_gather x1, waiting for transfers between devices, micro_pass(): lax.all_gather(shards[7], 'fsdp', axis=0, tiled=True)  51.6 us
    all_gather x1, waiting for transfers between devices, micro_pass(): lax.all_gather(shards[9], 'fsdp', axis=0, tiled=True)  50.5 us
    reshape x5, local copies, waits for them, and re-layouts, body(): grad.reshape(owners, -1)  36.4 us
    all_gather x1, waiting for transfers between devices, micro_pass(): lax.all_gather(shards[2], 'fsdp', axis=0, tiled=True)  36.1 us
  transfers between devices with their start and end apart: 14, of which 11 were waited for; matrix products, arithmetic and copies ran while one was open for 9% of the time, Pallas kernels for 0%

commit v1 on v0

v1 whole, which is shorter than its diff:
```python
import jax
import jax.numpy as jnp
from jax import lax
from jax.sharding import PartitionSpec as P

D = 768
H = 12
HD = 64


eps = 1e-06


def normalize(values):
    centered = values - jnp.mean(values, axis=-1, keepdims=True)
    inverse = lax.rsqrt(jnp.mean(centered * centered, axis=-1, keepdims=True) + eps)
    return (centered * inverse, inverse)


def norm_back(grad_in, normed, inverse):
    return inverse * (
        grad_in
        - jnp.mean(grad_in, axis=-1, keepdims=True)
        - normed * jnp.mean(grad_in * normed, axis=-1, keepdims=True)
    )


def gelu_tanh(values):
    return jax.nn.gelu(values, approximate=True)


def silu_back(values, grad_out):
    return jax.vjp(jax.nn.silu, values)[1](grad_out)[0]


def gelu_back(values, grad_out):
    return jax.vjp(gelu_tanh, values)[1](grad_out)[0]


LANES = 2048


def reduce_rows(grad):
    return lax.psum_scatter(
        grad.astype(jnp.bfloat16), ("fsdp", "sp"), scatter_dimension=0, tiled=True
    ).astype(jnp.float32)


def body(
    latents,
    condition,
    cotangent,
    w_ada,
    b_ada,
    w_qkv,
    b_query,
    b_value,
    w_out,
    b_out,
    w_up,
    b_up,
    w_down,
    b_down,
):
    f32 = jnp.float32
    bf16 = jnp.bfloat16
    fsdp_count = lax.axis_size("fsdp")
    sp_count = lax.axis_size("sp")
    owners = fsdp_count * sp_count
    fsdp_index = lax.axis_index("fsdp")
    sp_index = lax.axis_index("sp")
    owner_index = fsdp_index * sp_count + sp_index
    pair_latents = latents.shape[0]
    own_latents = pair_latents // sp_count
    latent_total = pair_latents * fsdp_count
    tokens_all = latents.shape[1] * sp_count
    scale_factor = HD ** (-0.5)

    small = [condition.reshape(-1), b_ada, b_query, b_value, b_out, b_up, b_down]
    width = sum(part.size for part in small)
    padded = -(-width // LANES) * LANES
    small.append(jnp.zeros((padded - width,), bf16))
    small_all = lax.all_gather(
        jnp.concatenate(small).reshape(1, padded // 128, 128), "fsdp", axis=0, tiled=True
    ).reshape(fsdp_count, padded)
    pieces = []
    start = 0
    for part in small[:-1]:
        pieces.append(small_all[:, start : start + part.size].reshape(-1))
        start = start + part.size
    cond_all, ada_bias, query_bias, value_bias, out_bias, up_bias, down_bias = pieces
    cond_all = cond_all.reshape(latent_total, D).astype(f32)
    silu_all = jax.nn.silu(cond_all)

    inputs = lax.all_to_all(latents, "sp", split_axis=0, concat_axis=1, tiled=True).astype(f32)
    grad_out = lax.all_to_all(cotangent, "sp", split_axis=0, concat_axis=1, tiled=True).astype(f32)

    ada_rows = w_ada.shape[0]
    silu_mine = lax.dynamic_index_in_dim(
        silu_all.astype(bf16).reshape(fsdp_count, sp_count, own_latents, D), sp_index, 1, False
    )
    silu_mine = lax.dynamic_index_in_dim(
        silu_mine.reshape(fsdp_count * own_latents, fsdp_count, ada_rows), fsdp_index, 1, False
    )
    mod_part = jnp.dot(silu_mine, w_ada, preferred_element_type=f32)
    mod_part = lax.all_to_all(
        mod_part.reshape(fsdp_count, own_latents * 6 * D), "fsdp", split_axis=0, concat_axis=0, tiled=True
    )
    modulate = jnp.sum(mod_part, axis=0).reshape(own_latents, 6 * D) + ada_bias.astype(f32)
    mod_parts = modulate.reshape(own_latents, 6, 1, D)
    shift_one, scale_one, gate_one = (mod_parts[:, 0], mod_parts[:, 1], mod_parts[:, 2])
    shift_two, scale_two, gate_two = (mod_parts[:, 3], mod_parts[:, 4], mod_parts[:, 5])

    qkv_full = lax.all_gather(w_qkv, "fsdp", axis=0, tiled=True)
    out_full = lax.all_gather(w_out, "fsdp", axis=0, tiled=True)
    up_full = lax.all_gather(w_up, "fsdp", axis=0, tiled=True)
    down_full = lax.all_gather(w_down, "fsdp", axis=0, tiled=True)

    normed_one, inverse_one = normalize(inputs)
    attn_in = (normed_one * (1.0 + scale_one) + shift_one).astype(bf16)
    qkv_bias = jnp.concatenate([query_bias, jnp.zeros_like(query_bias), value_bias]).astype(f32)
    projected = (
        jnp.einsum("btd,de->bte", attn_in, qkv_full, preferred_element_type=f32) + qkv_bias
    ).astype(bf16)
    heads = projected.reshape(own_latents, tokens_all, 3, H, HD).transpose(2, 0, 3, 1, 4)
    queries, key_heads, value_heads = heads[0], heads[1], heads[2]
    scores = (
        jnp.einsum("bhqd,bhkd->bhqk", queries, key_heads, preferred_element_type=f32) * scale_factor
    )
    log_total = jnp.log(jnp.sum(jnp.exp(scores), axis=-1, keepdims=True))
    soft_float = jnp.exp(scores - log_total)
    soft_half = soft_float.astype(bf16)
    mixed = jnp.einsum("bhqk,bhkd->bhqd", soft_half, value_heads, preferred_element_type=f32).astype(
        bf16
    )
    mixed_tokens = mixed.transpose(0, 2, 1, 3).reshape(own_latents, tokens_all, D)
    attn_proj = jnp.einsum(
        "btd,de->bte", mixed_tokens, out_full, preferred_element_type=f32
    ) + out_bias.astype(f32)
    residual = inputs + gate_one * attn_proj
    normed_two, inverse_two = normalize(residual)
    mlp_in = (normed_two * (1.0 + scale_two) + shift_two).astype(bf16)
    up_value = jnp.einsum(
        "btd,df->btf", mlp_in, up_full, preferred_element_type=f32
    ) + up_bias.astype(f32)
    activated = gelu_tanh(up_value).astype(bf16)
    down_value = jnp.einsum(
        "btf,fd->btd", activated, down_full, preferred_element_type=f32
    ) + down_bias.astype(f32)
    output = (residual + gate_two * down_value).astype(bf16)
    output = lax.all_to_all(output, "sp", split_axis=1, concat_axis=0, tiled=True)

    grad_gate_two = jnp.sum(grad_out * down_value, axis=1)
    grad_down = (grad_out * gate_two).astype(bf16)
    gw_down = jnp.einsum("btf,btd->fd", activated, grad_down, preferred_element_type=f32)
    own_down = reduce_rows(gw_down)
    gb_down = jnp.sum(grad_down.astype(f32), axis=(0, 1))
    grad_act = jnp.einsum("btd,fd->btf", grad_down, down_full, preferred_element_type=f32)
    grad_up = gelu_back(up_value, grad_act).astype(bf16)
    gw_up = jnp.einsum("btd,btf->df", mlp_in, grad_up, preferred_element_type=f32)
    own_up = reduce_rows(gw_up)
    gb_up = jnp.sum(grad_up.astype(f32), axis=(0, 1))
    grad_mlp = jnp.einsum("btf,df->btd", grad_up, up_full, preferred_element_type=f32)
    grad_scale_two = jnp.sum(grad_mlp * normed_two, axis=1)
    grad_shift_two = jnp.sum(grad_mlp, axis=1)
    grad_resid = grad_out + norm_back(grad_mlp * (1.0 + scale_two), normed_two, inverse_two)
    grad_gate_one = jnp.sum(grad_resid * attn_proj, axis=1)
    grad_proj = (grad_resid * gate_one).astype(bf16)
    gw_out = jnp.einsum("btd,bte->de", mixed_tokens, grad_proj, preferred_element_type=f32)
    own_out = reduce_rows(gw_out)
    gb_out = jnp.sum(grad_proj.astype(f32), axis=(0, 1))
    grad_mixed = jnp.einsum("bte,de->btd", grad_proj, out_full, preferred_element_type=f32).astype(
        bf16
    )
    grad_heads = grad_mixed.reshape(own_latents, tokens_all, H, HD).transpose(0, 2, 1, 3)
    grad_soft = jnp.einsum("bhqd,bhkd->bhqk", grad_heads, value_heads, preferred_element_type=f32)
    delta_sum = jnp.sum(soft_float * grad_soft, axis=-1, keepdims=True)
    grad_scores = (soft_float * (grad_soft - delta_sum)).astype(bf16)
    grad_queries = (
        jnp.einsum("bhqk,bhkd->bhqd", grad_scores, key_heads, preferred_element_type=f32)
        * scale_factor
    ).astype(bf16)
    grad_keys = (
        jnp.einsum("bhqk,bhqd->bhkd", grad_scores, queries, preferred_element_type=f32)
        * scale_factor
    ).astype(bf16)
    grad_values = jnp.einsum(
        "bhqk,bhqd->bhkd", soft_half, grad_heads, preferred_element_type=f32
    ).astype(bf16)
    grad_tokens = (
        jnp.stack([grad_queries, grad_keys, grad_values], axis=0)
        .transpose(1, 3, 0, 2, 4)
        .reshape(own_latents, tokens_all, 3 * D)
    )
    gw_qkv = jnp.einsum("btd,bte->de", attn_in, grad_tokens, preferred_element_type=f32)
    own_qkv = reduce_rows(gw_qkv)
    grad_tok_float = grad_tokens.astype(f32)
    gb_query = jnp.sum(grad_tok_float[:, :, :D], axis=(0, 1))
    gb_value = jnp.sum(grad_tok_float[:, :, 2 * D :], axis=(0, 1))
    grad_attn_in = jnp.einsum("bte,de->btd", grad_tokens, qkv_full, preferred_element_type=f32)
    grad_scale_one = jnp.sum(grad_attn_in * normed_one, axis=1)
    grad_shift_one = jnp.sum(grad_attn_in, axis=1)
    grad_latents = grad_resid + norm_back(grad_attn_in * (1.0 + scale_one), normed_one, inverse_one)
    grad_latents = lax.all_to_all(grad_latents, "sp", split_axis=1, concat_axis=0, tiled=True)

    grad_small = [
        grad_shift_one.reshape(-1),
        grad_scale_one.reshape(-1),
        grad_gate_one.reshape(-1),
        grad_shift_two.reshape(-1),
        grad_scale_two.reshape(-1),
        grad_gate_two.reshape(-1),
        gb_query,
        gb_value,
        gb_out,
        gb_up,
        gb_down,
    ]
    grad_small_all = lax.all_gather(jnp.concatenate(grad_small), ("fsdp", "sp"), axis=0)
    mod_width = 6 * own_latents * D
    grad_mod = (
        grad_small_all[:, :mod_width]
        .reshape(owners, 6, own_latents, D)
        .transpose(0, 2, 1, 3)
        .reshape(latent_total, 6 * D)
    )
    bias_sums = jnp.sum(grad_small_all[:, mod_width:], axis=0)
    own_bias = []
    start = 0
    for part in grad_small[6:]:
        piece = bias_sums[start : start + part.size].reshape(owners, -1)
        own_bias.append(lax.dynamic_index_in_dim(piece, owner_index, 0, False))
        start = start + part.size
    own_gb_query, own_gb_value, own_gb_out, own_gb_up, own_gb_down = own_bias
    silu_rows = lax.dynamic_index_in_dim(
        silu_all.reshape(latent_total, owners, D // owners), owner_index, 1, False
    )
    own_ada = jnp.dot(silu_rows.T, grad_mod, precision=lax.Precision.HIGHEST)
    own_gb_ada = lax.dynamic_index_in_dim(
        jnp.sum(grad_mod, axis=0).reshape(owners, -1), owner_index, 0, False
    )
    grad_silu = jnp.dot(grad_mod.astype(bf16), w_ada.T, preferred_element_type=f32)
    grad_silu = lax.all_to_all(
        grad_silu.reshape(fsdp_count, pair_latents * ada_rows),
        "fsdp",
        split_axis=0,
        concat_axis=0,
        tiled=True,
    )
    grad_silu = (
        grad_silu.reshape(fsdp_count, pair_latents, ada_rows)
        .transpose(1, 0, 2)
        .reshape(pair_latents, D)
    )
    grad_condition = silu_back(condition.astype(f32), grad_silu)
    return (
        output,
        grad_latents,
        grad_condition,
        own_ada,
        own_gb_ada,
        own_qkv,
        own_gb_query,
        own_gb_value,
        own_out,
        own_gb_out,
        own_up,
        own_gb_up,
        own_down,
        own_gb_down,
    )


def solution(mesh):
    in_specs = (
        P("fsdp", "sp", None),
        P("fsdp", None),
        P("fsdp", "sp", None),
        P("fsdp", None),
        P("fsdp"),
        P("fsdp", None),
        P("fsdp"),
        P("fsdp"),
        P("fsdp", None),
        P("fsdp"),
        P("fsdp", None),
        P("fsdp"),
        P("fsdp", None),
        P("fsdp"),
    )
    out_specs = (
        P("fsdp", "sp", None),
        P("fsdp", "sp", None),
        P("fsdp", None),
        P(("fsdp", "sp"), None),
        P(("fsdp", "sp")),
        P(("fsdp", "sp"), None),
        P(("fsdp", "sp")),
        P(("fsdp", "sp")),
        P(("fsdp", "sp"), None),
        P(("fsdp", "sp")),
        P(("fsdp", "sp"), None),
        P(("fsdp", "sp")),
        P(("fsdp", "sp"), None),
        P(("fsdp", "sp")),
    )
    return jax.shard_map(body, mesh=mesh, in_specs=in_specs, out_specs=out_specs, check_vma=False)
```

time: 1310 us -> 745 us (0.57)
  local copies, waits for them, and re-layouts: 231 us -> 29.6 us
  waiting for transfers between devices: 770 us -> 570 us
  matrix products: 126 us -> 60.4 us
  blocking collectives: 84.2 us -> 22.7 us
  other arithmetic: 38 us -> 23 us
    unnamed x7 -> x9, waiting for transfers between devices: 592 us -> 2.66 us
    reduce_scatter x0 -> x4, waiting for transfers between devices: none -> 355 us  [reduce_rows(): lax.psum_scatter(grad.astype(jnp.bfloat16), ('fsdp', 'sp'), scatter_dimen...]
    unnamed x223 -> x52, local copies, waits for them, and re-layouts: 126 us -> 12.9 us
    unnamed x1 -> x0, blocking collectives: 65.8 us -> none
    dot_general x40 -> x21, matrix products: 126 us -> 60.4 us  [the longest x1 7.03 us: body(): jnp.einsum('btd,df->btf', mlp_in, up_full, preferred_element_type=f32)]
    reshape x22 -> x6, local copies, waits for them, and re-layouts: 53.7 us -> 1.13 us  [the longest x1 0.7 us: body(): condition.reshape(-1)]
    all_gather x5, waiting for transfers between devices: 146 us -> 174 us  [the longest x1 55.6 us: body(): lax.all_gather(jnp.concatenate(grad_small), ('fsdp', 'sp'), axis=0)]
    all_gather x0 -> x1, blocking collectives: none -> 22.7 us  [body(): lax.all_gather(jnp.concatenate(small).reshape(1, padded // 128, 128), 'fs...]
  transfers between devices with their start and end apart: 14 -> 15, of which waited for: 11 -> 13; matrix products, arithmetic and copies ran while one was open for 9% -> 9% of each run, Pallas kernels for 0% -> 0%
where the time goes in v1:
time: 745 us; the launch traced here: 744 us
  waiting for transfers between devices  570 us (77%)
  matrix products  60.4 us (8%)
  local copies, waits for them, and re-layouts  29.6 us (4%)
  starting transfers between devices  23.8 us (3%)
  other arithmetic  23 us (3%)
  blocking collectives  22.7 us (3%)
  between operations  14.4 us (2%)
    reduce_scatter x4, waiting for transfers between devices, reduce_rows(): lax.psum_scatter(grad.astype(jnp.bfloat16), ('fsdp', 'sp'), scatter_dimen...  355 us
    all_gather x1, waiting for transfers between devices, body(): lax.all_gather(jnp.concatenate(grad_small), ('fsdp', 'sp'), axis=0)  55.6 us
    all_gather x1, waiting for transfers between devices, body(): down_full = lax.all_gather(w_down, 'fsdp', axis=0, tiled=True)  51.3 us
    all_gather x1, waiting for transfers between devices, body(): up_full = lax.all_gather(w_up, 'fsdp', axis=0, tiled=True)  48.3 us
    all_gather x1, blocking collectives, body(): lax.all_gather(jnp.concatenate(small).reshape(1, padded // 128, 128), 'fs...  22.7 us
    all_gather x1, waiting for transfers between devices, body(): out_full = lax.all_gather(w_out, 'fsdp', axis=0, tiled=True)  18.5 us
  transfers between devices with their start and end apart: 15, of which 13 were waited for; matrix products, arithmetic and copies ran while one was open for 9% of the time, Pallas kernels for 0%

profile of v1, /device:TPU:0, one launch (start us, length us, event | category | flops | bytes accessed | tf_op | source)
XLA Modules:
  0.0 743.5 jit_solution(2040132775007080298)
XLA Ops:
  10.0 4.2 all-to-all-start
  14.9 4.1 concatenate.17
  19.1 22.7 %all_gather.21 = bf16[16,32,128]{2,1,0:T(8,128)(2,1)S(1)} all-gather(bf16[1,32,128]{2,1,0:T(8,128)(2,1)S(1)} %bitcast.185), channel_id=1, replica_groups=mesh['fsdp'=16,'sp'=2] {'fsdp'}, dimensions={0}, use_global_device_ids=true | all-gather | bytes 139264 | tf_op jit(solution)/shard_map/all_gather | solution.py:83
  43.7 3.5 all-to-all-start.1
  48.0 13.6 %all-to-all-done.1 = f32[16,1,4608]{2,1,0:T(1,128)S(1)} async-done(((f32[16,1,4608]{2,1,0:T(1,128)}), f32[16,1,4608]{2,1,0:T(1,128)S(1)}, u32[]{:S(2)}, u32[]{:S(2)}) %all-to-all-start.1) | async-done | bytes 294944 | tf_op jit(solution)/shard_map/all_to_all | solution.py:106
  61.7 3.8 all-to-all-start.3
  65.8 6.4 all-to-all-done.3
  73.4 4.2 fusion.1
  77.6 1.6 copy.62
  79.1 2.3 fusion.55
  81.4 4.8 convolution_convert_fusion.4
  86.2 18.5 %all-gather.10.cloned.1.call-done = bf16[768,768]{1,0:T(8,128)(2,1)} async-done(((bf16[48,768]{1,0:T(8,128)(2,1)}), bf16[768,768]{1,0:T(8,128)(2,1)}) %all-gather.10.cloned.1.call-update) | async-done | bytes 1179664 | tf_op jit(solution)/shard_map/all_gather | solution.py:115
  104.6 2.8 fusion.81
  107.7 51.3 %all-gather.14.cloned.1.call-done = bf16[3072,768]{1,0:T(8,128)(2,1)} async-done(((bf16[192,768]{1,0:T(8,128)(2,1)}), bf16[3072,768]{1,0:T(8,128)(2,1)}) %all-gather.14.cloned.1.call-update) | async-done | bytes 4718608 | tf_op jit(solution)/shard_map/all_gather | solution.py:117
  159.0 5.5 fusion.83
  164.5 48.3 %all-gather.12.cloned.1.call-done = bf16[768,3072]{1,0:T(8,128)(2,1)} async-done(((bf16[48,3072]{1,0:T(8,128)(2,1)}), bf16[768,3072]{1,0:T(8,128)(2,1)}) %all-gather.12.cloned.1.call-update) | async-done | bytes 4718608 | tf_op jit(solution)/shard_map/all_gather | solution.py:116
  212.8 7.0 convert_reduce_fusion
  219.9 1.8 multiply_reduce_fusion.1
  222.2 1.7 copy-done.3
  223.9 3.2 fusion.22
  229.3 4.8 fusion.17
  236.0 2.9 multiply_reduce_fusion
  242.0 1.5 convolution_convert_fusion.3
  243.5 1.4 pad_maximum_fusion
  244.9 4.2 fusion.36
  249.0 1.6 convert.10
  250.7 3.0 multiply_reduce_fusion.2
  255.1 2.9 convolution_convert_fusion.2
  258.1 1.3 copy-done.8
  259.5 3.7 convolution_convert_fusion.1
  264.1 6.3 convolution_convert_fusion
  272.6 3.0 reduce.57
  276.5 3.5 all-to-all-start.2
  279.9 1.7 copy.70
  281.6 5.5 all-to-all-done.2
  287.2 3.5 all-to-all-start.4
  292.4 11.1 %all-to-all-done.4 = f32[1,256,768]{2,0,1:T(1,128)S(1)} async-done(((f32[1,256,768]{2,0,1:T(1,128)}), f32[1,256,768]{2,0,1:T(1,128)S(1)}, u32[]{:S(2)}, u32[]{:S(2)}) %all-to-all-start.4) | async-done | bytes 786464 | tf_op jit(solution)/shard_map/all_to_all | solution.py:204
  304.4 42.0 %reduce-scatter.7.cloned.1.call-done = bf16[24,768]{1,0:T(8,128)(2,1)} async-done(((bf16[768,768]{1,0:T(8,128)(2,1)}), bf16[24,768]{1,0:T(8,128)(2,1)}) %reduce-scatter.7.cloned.1.call-update) | async-done | bytes 36880 | tf_op jit(solution)/shard_map/reduce_scatter | solution.py:44
  346.3 1.4 convert_element_type.318
  347.7 55.6 %all-gather.16.cloned.1.call-done = f32[32,1,10752]{2,1,0:T(1,128)} async-done(((f32[1,1,10752]{2,1,0:T(1,128)}), f32[32,1,10752]{2,1,0:T(1,128)}) %all-gather.16.cloned.1.call-update) | async-done | bytes 1376272 | tf_op jit(solution)/shard_map/all_gather | solution.py:219
  403.3 1.4 copy.91
  405.7 4.6 all-to-all-start.5
  418.6 92.5 %reduce-scatter.5.cloned.1.call-done = bf16[24,2304]{1,0:T(8,128)(2,1)} async-done(((bf16[768,2304]{1,0:T(8,128)(2,1)}), bf16[24,2304]{1,0:T(8,128)(2,1)}) %reduce-scatter.5.cloned.1.call-update) | async-done | bytes 110608 | tf_op jit(solution)/shard_map/reduce_scatter | solution.py:44
  511.1 1.6 convert_element_type.316
  512.7 110.3 %reduce-scatter.9.cloned.1.call-done = bf16[24,3072]{1,0:T(8,128)(2,1)} async-done(((bf16[768,3072]{1,0:T(8,128)(2,1)}), bf16[24,3072]{1,0:T(8,128)(2,1)}) %reduce-scatter.9.cloned.1.call-update) | async-done | bytes 147472 | tf_op jit(solution)/shard_map/reduce_scatter | solution.py:44
  623.0 1.6 convert_element_type.320
  624.6 110.7 %reduce-scatter.11.cloned.1.call-done = bf16[96,768]{1,0:T(8,128)(2,1)} async-done(((bf16[3072,768]{1,0:T(8,128)(2,1)}), bf16[96,768]{1,0:T(8,128)(2,1)}) %reduce-scatter.11.cloned.1.call-update) | async-done | bytes 147472 | tf_op jit(solution)/shard_map/reduce_scatter | solution.py:44
  735.3 1.6 convert_element_type.322
  (147 shorter events, 32.5 us)
Async XLA Ops:
  7.2 35.0 %copy-start = (bf16[48,4608]{1,0:T(8,128)(2,1)S(1)}, bf16[48,4608]{1,0:T(8,128)(2,1)}, u32[]{:S(2)}) copy-start(bf16[48,4608]{1,0:T(8,128)(2,1)} %param.17) | copy-start | bytes 1327108
  7.2 66.2 %all-gather.8.cloned.1.call-start = ((), (), s32[]{:S(2)}) async-start(), calls=%async_computation.10 | async-start | bytes 3760128 | tf_op jit(solution)/shard_map/all_gather | solution.py:114
  7.9 96.7 %all-gather.10.cloned.1.call-start = ((), (), s32[]{:S(2)}) async-start(), calls=%async_computation.11 | async-start | bytes 1253376 | tf_op jit(solution)/shard_map/all_gather | solution.py:115
  8.7 150.3 %all-gather.14.cloned.1.call-start = ((), (), s32[]{:S(2)}) async-start(), calls=%async_computation.13 | async-start | bytes 5013504 | tf_op jit(solution)/shard_map/all_gather | solution.py:117
  9.4 203.4 %all-gather.12.cloned.1.call-start = ((), (), s32[]{:S(2)}) async-start(), calls=%async_computation.12 | async-start | bytes 5013504 | tf_op jit(solution)/shard_map/all_gather | solution.py:116
  10.0 33.7 %all-to-all-start = ((bf16[2,128,768]{2,1,0:T(8,128)(2,1)}), bf16[2,128,768]{2,1,0:T(8,128)(2,1)S(1)}, u32[]{:S(2)}, u32[]{:S(2)}) async-start(bf16[2,128,768]{2,1,0:T(8,128)(2,1)} %param.14), calls=%async_computation | async-start | bytes 786432 | tf_op jit(solution)/shard_map/all_to_all | solution.py:95
  43.7 17.9 %all-to-all-start.1 = ((f32[16,1,4608]{2,1,0:T(1,128)}), f32[16,1,4608]{2,1,0:T(1,128)S(1)}, u32[]{:S(2)}, u32[]{:S(2)}) async-start(f32[16,1,4608]{2,1,0:T(1,128)} %copy.61), calls=%async_computation.1 | async-start | bytes 589824 | tf_op jit(solution)/shard_map/all_to_all | solution.py:106
  61.7 10.5 %all-to-all-start.3 = ((bf16[2,128,768]{2,1,0:T(8,128)(2,1)}), bf16[2,128,768]{2,1,0:T(8,128)(2,1)S(1)}, u32[]{:S(2)}, u32[]{:S(2)}) async-start(bf16[2,128,768]{2,1,0:T(8,128)(2,1)} %param.16), calls=%async_computation.3 | async-start | bytes 786432 | tf_op jit(solution)/shard_map/all_to_all | solution.py:96
  65.5 280.9 %reduce-scatter.7.cloned.1.call-start = ((), (), s32[]{:S(2)}) async-start(), calls=%async_computation.15 | async-start | bytes 1216512 | tf_op jit(solution)/shard_map/reduce_scatter | solution.py:44
  212.8 7.1 copy-start.15
  219.8 1.8 copy-start.7
  219.8 2.4 copy-start.16
  219.9 4.0 copy-start.3
  223.9 3.9 copy-start.4
  227.1 0.7 copy-start.10
  229.3 4.8 copy-start.12
  234.1 1.9 copy-start.1
  239.5 2.5 copy-start.9
  239.5 2.5 copy-start.11
  250.7 152.7 %all-gather.16.cloned.1.call-start = ((), (), s32[]{:S(2)}) async-start(), calls=%async_computation.18 | async-start | bytes 1419264 | tf_op jit(solution)/shard_map/all_gather | solution.py:219
  250.7 3.1 copy-start.2
  254.8 256.3 %reduce-scatter.5.cloned.1.call-start = ((), (), s32[]{:S(2)}) async-start(), calls=%async_computation.14 | async-start | bytes 3649536 | tf_op jit(solution)/shard_map/reduce_scatter | solution.py:44
  258.0 1.4 copy-start.8
  258.1 364.9 %reduce-scatter.9.cloned.1.call-start = ((), (), s32[]{:S(2)}) async-start(), calls=%async_computation.16 | async-start | bytes 4866048 | tf_op jit(solution)/shard_map/reduce_scatter | solution.py:44
  263.2 1.0 copy-start.6
  263.2 472.2 %reduce-scatter.11.cloned.1.call-start = ((), (), s32[]{:S(2)}) async-start(), calls=%async_computation.17 | async-start | bytes 4866048 | tf_op jit(solution)/shard_map/reduce_scatter | solution.py:44
  270.5 1.0 copy-start.13
  270.5 9.4 %copy-start.5 = (f32[256,768]{1,0:T(8,128)S(1)}, f32[256,768]{1,0:T(8,128)}, u32[]{:S(2)}) copy-start(f32[256,768]{1,0:T(8,128)} %get-tuple-element.43) | copy-start | bytes 2359300
  276.5 10.7 %all-to-all-start.2 = ((bf16[2,2,49152]{2,1,0:T(2,128)(2,1)}), bf16[2,2,49152]{2,1,0:T(2,128)(2,1)S(1)}, u32[]{:S(2)}, u32[]{:S(2)}) async-start(bf16[2,2,49152]{2,1,0:T(2,128)(2,1)} %reshape.788), calls=%async_computation.2 | async-start | bytes 786432 | tf_op jit(solution)/shard_map/all_to_all | solution.py:151
  287.2 16.3 %all-to-all-start.4 = ((f32[1,256,768]{2,0,1:T(1,128)}), f32[1,256,768]{2,0,1:T(1,128)S(1)}, u32[]{:S(2)}, u32[]{:S(2)}) async-start(f32[1,256,768]{2,0,1:T(1,128)} %copy.70), calls=%async_computation.4 | async-start | bytes 1572864 | tf_op jit(solution)/shard_map/all_to_all | solution.py:204
  347.7 70.2 %copy-start.14 = (bf16[2,768]{1,0:T(2,128)(2,1)S(1)}, bf16[2,768]{1,0:T(2,128)(2,1)}, u32[]{:S(2)}) copy-start(bf16[2,768]{1,0:T(2,128)(2,1)} %param.15) | copy-start | bytes 9220
  405.7 11.0 %all-to-all-start.5 = ((f32[16,1,96]{2,1,0:T(1,128)}), f32[16,1,96]{2,1,0:T(1,128)S(1)}, u32[]{:S(2)}, u32[]{:S(2)}) async-start(f32[16,1,96]{2,1,0:T(1,128)} %bitcast.31), calls=%async_computation.5 | async-start | bytes 16384 | tf_op jit(solution)/shard_map/all_to_all | solution.py:243
Sparse Core Ops, SparseCore 0:
  10.3 55.0 all-gather.7
  67.7 36.8 all-gather.9
  106.9 51.9 all-gather.13
  161.1 51.6 all-gather.11
  250.8 95.5 reduce-scatter.6
  349.6 53.6 all-gather.15
  408.7 102.3 reduce-scatter.4
  516.6 106.3 reduce-scatter.8
  628.5 106.8 reduce-scatter.10

commit v2 on v1

--- a/solution.py
+++ b/solution.py
@@ -38,12 +38,6 @@
 
 
 LANES = 2048
-
-
-def reduce_rows(grad):
-    return lax.psum_scatter(
-        grad.astype(jnp.bfloat16), ("fsdp", "sp"), scatter_dimension=0, tiled=True
-    ).astype(jnp.float32)
 
 
 def body(
@@ -153,12 +147,10 @@
     grad_gate_two = jnp.sum(grad_out * down_value, axis=1)
     grad_down = (grad_out * gate_two).astype(bf16)
     gw_down = jnp.einsum("btf,btd->fd", activated, grad_down, preferred_element_type=f32)
-    own_down = reduce_rows(gw_down)
     gb_down = jnp.sum(grad_down.astype(f32), axis=(0, 1))
     grad_act = jnp.einsum("btd,fd->btf", grad_down, down_full, preferred_element_type=f32)
     grad_up = gelu_back(up_value, grad_act).astype(bf16)
     gw_up = jnp.einsum("btd,btf->df", mlp_in, grad_up, preferred_element_type=f32)
-    own_up = reduce_rows(gw_up)
     gb_up = jnp.sum(grad_up.astype(f32), axis=(0, 1))
     grad_mlp = jnp.einsum("btf,df->btd", grad_up, up_full, preferred_element_type=f32)
     grad_scale_two = jnp.sum(grad_mlp * normed_two, axis=1)
@@ -167,7 +159,6 @@
     grad_gate_one = jnp.sum(grad_resid * attn_proj, axis=1)
     grad_proj = (grad_resid * gate_one).astype(bf16)
     gw_out = jnp.einsum("btd,bte->de", mixed_tokens, grad_proj, preferred_element_type=f32)
-    own_out = reduce_rows(gw_out)
     gb_out = jnp.sum(grad_proj.astype(f32), axis=(0, 1))
     grad_mixed = jnp.einsum("bte,de->btd", grad_proj, out_full, preferred_element_type=f32).astype(
         bf16
@@ -193,7 +184,6 @@
         .reshape(own_latents, tokens_all, 3 * D)
     )
     gw_qkv = jnp.einsum("btd,bte->de", attn_in, grad_tokens, preferred_element_type=f32)
-    own_qkv = reduce_rows(gw_qkv)
     grad_tok_float = grad_tokens.astype(f32)
     gb_query = jnp.sum(grad_tok_float[:, :, :D], axis=(0, 1))
     gb_value = jnp.sum(grad_tok_float[:, :, 2 * D :], axis=(0, 1))
@@ -203,34 +193,63 @@
     grad_latents = grad_resid + norm_back(grad_attn_in * (1.0 + scale_one), normed_one, inverse_one)
     grad_latents = lax.all_to_all(grad_latents, "sp", split_axis=1, concat_axis=0, tiled=True)
 
-    grad_small = [
-        grad_shift_one.reshape(-1),
-        grad_scale_one.reshape(-1),
-        grad_gate_one.reshape(-1),
-        grad_shift_two.reshape(-1),
-        grad_scale_two.reshape(-1),
-        grad_gate_two.reshape(-1),
-        gb_query,
-        gb_value,
-        gb_out,
-        gb_up,
-        gb_down,
-    ]
-    grad_small_all = lax.all_gather(jnp.concatenate(grad_small), ("fsdp", "sp"), axis=0)
-    mod_width = 6 * own_latents * D
-    grad_mod = (
-        grad_small_all[:, :mod_width]
-        .reshape(owners, 6, own_latents, D)
+    grad_mod = jnp.concatenate(
+        [
+            grad_shift_one,
+            grad_scale_one,
+            grad_gate_one,
+            grad_shift_two,
+            grad_scale_two,
+            grad_gate_two,
+        ],
+        axis=1,
+    )
+    grad_mod = lax.all_to_all(
+        jnp.broadcast_to(grad_mod[None], (owners, own_latents, 6 * D)),
+        ("fsdp", "sp"),
+        split_axis=0,
+        concat_axis=0,
+        tiled=True,
+    ).reshape(latent_total, 6 * D)
+
+    rows = D // owners
+    biases = (gb_query, gb_value, gb_out, gb_up, gb_down)
+    bias_rows = jnp.concatenate([part.reshape(owners, -1) for part in biases], axis=1)
+    bias_width = bias_rows.shape[1]
+    bias_lanes = -(-bias_width // (rows * 128)) * 128
+    bias_rows = jnp.pad(bias_rows, ((0, 0), (0, rows * bias_lanes - bias_width)))
+    stack = down_full.shape[0] // D
+    gw_down = (
+        gw_down.astype(bf16)
+        .reshape(owners, stack, rows, D)
         .transpose(0, 2, 1, 3)
-        .reshape(latent_total, 6 * D)
-    )
-    bias_sums = jnp.sum(grad_small_all[:, mod_width:], axis=0)
+        .reshape(D, stack * D)
+    )
+    packed = jnp.concatenate(
+        [
+            gw_down,
+            gw_up.astype(bf16),
+            gw_qkv.astype(bf16),
+            gw_out.astype(bf16),
+            bias_rows.astype(bf16).reshape(D, bias_lanes),
+        ],
+        axis=1,
+    )
+    owned = lax.psum_scatter(packed, ("fsdp", "sp"), scatter_dimension=0, tiled=True).astype(f32)
+    own_weights = []
+    start = 0
+    for width in (stack * D, up_full.shape[1], 3 * D, D, bias_lanes):
+        own_weights.append(owned[:, start : start + width])
+        start = start + width
+    own_down, own_up, own_qkv, own_out, bias_sums = own_weights
+    own_down = own_down.reshape(rows, stack, D).transpose(1, 0, 2).reshape(stack * rows, D)
+    bias_sums = bias_sums.reshape(-1)
     own_bias = []
     start = 0
-    for part in grad_small[6:]:
-        piece = bias_sums[start : start + part.size].reshape(owners, -1)
-        own_bias.append(lax.dynamic_index_in_dim(piece, owner_index, 0, False))
-        start = start + part.size
+    for part in biases:
+        width = part.size // owners
+        own_bias.append(bias_sums[start : start + width])
+        start = start + width
     own_gb_query, own_gb_value, own_gb_out, own_gb_up, own_gb_down = own_bias
     silu_rows = lax.dynamic_index_in_dim(
         silu_all.reshape(latent_total, owners, D // owners), owner_index, 1, False

time: 745 us -> 444 us (0.60)
  waiting for transfers between devices: 570 us -> 268 us
  local copies, waits for them, and re-layouts: 29.6 us -> 38.8 us
    reduce_scatter x4 -> x0, waiting for transfers between devices: 355 us -> none  [reduce_rows(): lax.psum_scatter(grad.astype(jnp.bfloat16), ('fsdp', 'sp'), scatter_dimen...]
    unnamed x9 -> x6, waiting for transfers between devices: 2.66 us -> 95.5 us
    all_gather x1 -> x0, waiting for transfers between devices: 55.6 us -> none  [body(): lax.all_gather(jnp.concatenate(grad_small), ('fsdp', 'sp'), axis=0)]
    all_to_all x0 -> x1, waiting for transfers between devices: none -> 18.4 us  [body(): lax.all_to_all(jnp.broadcast_to(grad_mod[None], (owners, own_latents, 6 *...]
  transfers between devices with their start and end apart: 15 -> 12, of which waited for: 13 -> 10; matrix products, arithmetic and copies ran while one was open for 9% -> 12% of each run, Pallas kernels for 0% -> 0%
where the time goes in v2:
time: 444 us; the launch traced here: 443 us
  waiting for transfers between devices  268 us (60%)
  matrix products  58 us (13%)
  local copies, waits for them, and re-layouts  38.8 us (9%)
  starting transfers between devices  24.9 us (6%)
  blocking collectives  22.7 us (5%)
  other arithmetic  16.2 us (4%)
  between operations  14.4 us (3%)
    unnamed x6, waiting for transfers between devices  95.5 us
    all_gather x1, waiting for transfers between devices, body(): down_full = lax.all_gather(w_down, 'fsdp', axis=0, tiled=True)  51.3 us
    all_gather x1, waiting for transfers between devices, body(): up_full = lax.all_gather(w_up, 'fsdp', axis=0, tiled=True)  48.2 us
    all_gather x1, blocking collectives, body(): lax.all_gather(jnp.concatenate(small).reshape(1, padded // 128, 128), 'fs...  22.7 us
    all_to_all x1, waiting for transfers between devices, body(): lax.all_to_all(jnp.broadcast_to(grad_mod[None], (owners, own_latents, 6 *...  18.4 us
    all_gather x1, waiting for transfers between devices, body(): out_full = lax.all_gather(w_out, 'fsdp', axis=0, tiled=True)  17.1 us
    all_to_all x1, waiting for transfers between devices, body(): lax.all_to_all(mod_part.reshape(fsdp_count, own_latents * 6 * D), 'fsdp',...  13.7 us
    unnamed x55, local copies, waits for them, and re-layouts  12.7 us
  transfers between devices with their start and end apart: 12, of which 10 were waited for; matrix products, arithmetic and copies ran while one was open for 12% of the time, Pallas kernels for 0%

profile of v2, /device:TPU:0, one launch (start us, length us, event | category | flops | bytes accessed | tf_op | source)
XLA Modules:
  0.0 443.4 jit_solution(5523221434767197551)
XLA Ops:
  10.0 4.2 all-to-all-start
  14.9 4.1 concatenate.24
  19.1 22.7 %all_gather.15 = bf16[16,32,128]{2,1,0:T(8,128)(2,1)S(1)} all-gather(bf16[1,32,128]{2,1,0:T(8,128)(2,1)S(1)} %bitcast.188), channel_id=1, replica_groups=mesh['fsdp'=16,'sp'=2] {'fsdp'}, dimensions={0}, use_global_device_ids=true | all-gather | bytes 139264 | tf_op jit(solution)/shard_map/all_gather | solution.py:77
  43.7 3.5 all-to-all-start.1
  48.0 13.7 %all-to-all-done.1 = f32[16,1,4608]{2,1,0:T(1,128)S(1)} async-done(((f32[16,1,4608]{2,1,0:T(1,128)}), f32[16,1,4608]{2,1,0:T(1,128)S(1)}, u32[]{:S(2)}, u32[]{:S(2)}) %all-to-all-start.1) | async-done | bytes 294944 | tf_op jit(solution)/shard_map/all_to_all | solution.py:100
  61.7 3.8 all-to-all-start.3
  65.8 6.4 %all-to-all-done.3 = bf16[2,128,768]{2,1,0:T(8,128)(2,1)S(1)} async-done(((bf16[2,128,768]{2,1,0:T(8,128)(2,1)}), bf16[2,128,768]{2,1,0:T(8,128)(2,1)S(1)}, u32[]{:S(2)}, u32[]{:S(2)}) %all-to-all-start.3) | async-done | bytes 393248 | tf_op jit(solution)/shard_map/all_to_all | solution.py:90
  74.5 4.1 fusion.3
  78.6 1.6 copy.105
  80.2 2.4 fusion.60
  82.6 4.9 %convolution_convert_fusion.4 = bf16[12,256,64]{1,2,0:T(8,128)(2,1)} fusion(f32[12,256,256]{1,2,0:T(8,128)} %fusion.60, bf16[3,1,12,256,64]{3,4,2,1,0:T(8,128)(2,1)S(1)} %bitcast.160), kind=kOutput, calls=%fused_computation.34 | convolution fusion | flops 104008960 | bytes 7077888 | tf_op jit(solution)/shard_map/bhqk,bhkd->bhqd/dot_general | solution.py:127
  87.4 17.1 %all-gather.7.cloned.1.call-done = bf16[768,768]{1,0:T(8,128)(2,1)} async-done(((bf16[48,768]{1,0:T(8,128)(2,1)}), bf16[768,768]{1,0:T(8,128)(2,1)}) %all-gather.7.cloned.1.call-update) | async-done | bytes 1179664 | tf_op jit(solution)/shard_map/all_gather | solution.py:109
  104.6 2.8 fusion.83
  107.6 51.3 %all-gather.11.cloned.1.call-done = bf16[3072,768]{1,0:T(8,128)(2,1)} async-done(((bf16[192,768]{1,0:T(8,128)(2,1)}), bf16[3072,768]{1,0:T(8,128)(2,1)}) %all-gather.11.cloned.1.call-update) | async-done | bytes 4718608 | tf_op jit(solution)/shard_map/all_gather | solution.py:111
  158.9 5.6 %fusion.86 = f32[256,3072]{1,0:T(8,128)} fusion(bf16[256,768]{1,0:T(8,128)(2,1)} %fusion.24, bf16[3072,768]{1,0:T(8,128)(2,1)} %all-gather.11.cloned.1.call-done), kind=kOutput, calls=%fused_computation.159 | convolution fusion | flops 1207959552 | bytes 8257536 | tf_op jit(solution)/shard_map/btd,fd->btf/dot_general | solution.py:151
  164.5 48.2 %all-gather.9.cloned.1.call-done = bf16[768,3072]{1,0:T(8,128)(2,1)} async-done(((bf16[48,3072]{1,0:T(8,128)(2,1)}), bf16[768,3072]{1,0:T(8,128)(2,1)}) %all-gather.9.cloned.1.call-update) | async-done | bytes 4718608 | tf_op jit(solution)/shard_map/all_gather | solution.py:110
  212.7 7.0 %fusion.80 = (bf16[3072]{0:T(1024)(128)(2,1)S(1)}, bf16[256,3072]{1,0:T(8,128)(2,1)S(1)}, f32[256,3072]{1,0:T(8,128)S(1)}) fusion(f32[256,3072]{1,0:T(8,128)} %fusion.86, f32[3072]{0:T(1024)S(1)} %reshape.760, bf16[768,3072]{1,0:T(8,128)(2,1)} %all-gather.9.cloned.1.call-done, f32[256,768]{1,0:T(8,128)S(1)} %get-tuple-element.36, ...), kind=kOutput, calls=%fused_computation.153 | convolution fusion | flops 1226241024 | bytes 13395968 | tf_op jit(solution)/shard_map/btd,df->btf/dot_general | solution.py:137
  219.8 1.4 fusion.87
  222.1 1.7 copy-done.2
  223.8 2.9 fusion.25
  226.7 1.3 fusion.82
  230.2 5.0 %fusion.20 = bf16[1,1,12,256,64]{3,4,2,1,0:T(8,128)(2,1)} fusion(bf16[12,256,64]{1,2,0:T(8,128)(2,1)} %bitcast.174, f32[12,256,256]{1,2,0:T(8,128)} %fusion.60), kind=kOutput, calls=%fused_computation.39 | convolution fusion | flops 104008960 | bytes 3932160 | tf_op jit(solution)/shard_map/bhqk,bhqd->bhkd/dot_general | solution.py:178
  235.8 1.3 copy-done.1
  237.1 2.9 multiply_reduce_fusion
  240.6 1.4 fusion.22
  241.9 1.1 fusion.21
  243.1 4.4 convolution_convert_fusion.2
  247.7 1.2 pad_maximum_fusion
  249.8 4.7 %copy.117 = bf16[32,24,4,768]{3,2,1,0:T(4,128)(2,1)S(1)} copy(bf16[32,24,4,768]{3,1,2,0:T(8,128)(2,1)} %bitcast.167) | data formatting | bytes 9437184 | tf_op jit(solution)/shard_map/transpose | solution.py:225
  255.6 2.5 constant_dynamic-update-slice_fusion.7
  258.0 3.7 fusion.2
  261.8 2.9 fusion.1
  264.7 1.6 fusion.17
  269.1 3.3 reduce.65
  273.2 3.6 all-to-all-start.2
  276.8 3.9 fusion.39
  281.1 1.7 copy.113
  282.8 1.2 all-to-all-done.2
  284.0 3.6 all-to-all-start.4
  287.7 10.6 %all-to-all-done.4 = f32[1,256,768]{2,0,1:T(1,128)S(1)} async-done(((f32[1,256,768]{2,0,1:T(1,128)}), f32[1,256,768]{2,0,1:T(1,128)S(1)}, u32[]{:S(2)}, u32[]{:S(2)}) %all-to-all-start.4) | async-done | bytes 786464 | tf_op jit(solution)/shard_map/all_to_all | solution.py:194
  299.4 2.6 all-to-all-start.5
  304.5 18.4 %all-to-all-done.5 = f32[32,1,4608]{2,1,0:T(1,128)S(1)} async-done(((f32[32,1,4608]{2,1,0:T(1,128)}), f32[32,1,4608]{2,1,0:T(1,128)S(1)}, u32[]{:S(2)}, u32[]{:S(2)}) %all-to-all-start.5) | async-done | bytes 589856 | tf_op jit(solution)/shard_map/all_to_all | solution.py:207
  323.9 3.5 all-to-all-start.6
  327.8 1.3 fusion.46
  329.7 6.0 %all-to-all-done.6 = f32[16,1,96]{2,1,0:T(1,128)S(1)} async-done(((f32[16,1,96]{2,1,0:T(1,128)}), f32[16,1,96]{2,1,0:T(1,128)S(1)}, u32[]{:S(2)}, u32[]{:S(2)}) %all-to-all-start.6) | async-done | bytes 6176 | tf_op jit(solution)/shard_map/all_to_all | solution.py:262
  337.6 92.9 %reduce-scatter.4.cloned.1.call-done = bf16[24,9344]{1,0:T(8,128)(2,1)} async-done(((bf16[768,9344]{1,0:T(8,128)(2,1)}), bf16[24,9344]{1,0:T(8,128)(2,1)}) %reduce-scatter.4.cloned.1.call-update) | async-done | bytes 448528
  430.5 1.1 convert_element_type.313
  432.8 1.7 fusion.84
  (144 shorter events, 30.4 us)
Async XLA Ops:
  7.2 35.3 %copy-start = (bf16[48,4608]{1,0:T(8,128)(2,1)S(1)}, bf16[48,4608]{1,0:T(8,128)(2,1)}, u32[]{:S(2)}) copy-start(bf16[48,4608]{1,0:T(8,128)(2,1)} %param.17) | copy-start | bytes 1327108
  7.2 67.3 %all-gather.5.cloned.1.call-start = ((), (), s32[]{:S(2)}) async-start(), calls=%async_computation.8 | async-start | bytes 3760128 | tf_op jit(solution)/shard_map/all_gather | solution.py:108
  7.9 96.6 %all-gather.7.cloned.1.call-start = ((), (), s32[]{:S(2)}) async-start(), calls=%async_computation.9 | async-start | bytes 1253376 | tf_op jit(solution)/shard_map/all_gather | solution.py:109
  8.7 150.2 %all-gather.11.cloned.1.call-start = ((), (), s32[]{:S(2)}) async-start(), calls=%async_computation.11 | async-start | bytes 5013504 | tf_op jit(solution)/shard_map/all_gather | solution.py:111
  9.4 203.3 %all-gather.9.cloned.1.call-start = ((), (), s32[]{:S(2)}) async-start(), calls=%async_computation.10 | async-start | bytes 5013504 | tf_op jit(solution)/shard_map/all_gather | solution.py:110
  10.0 33.7 %all-to-all-start = ((bf16[2,128,768]{2,1,0:T(8,128)(2,1)}), bf16[2,128,768]{2,1,0:T(8,128)(2,1)S(1)}, u32[]{:S(2)}, u32[]{:S(2)}) async-start(bf16[2,128,768]{2,1,0:T(8,128)(2,1)} %param.14), calls=%async_computation | async-start | bytes 786432 | tf_op jit(solution)/shard_map/all_to_all | solution.py:89
  43.7 18.0 %all-to-all-start.1 = ((f32[16,1,4608]{2,1,0:T(1,128)}), f32[16,1,4608]{2,1,0:T(1,128)S(1)}, u32[]{:S(2)}, u32[]{:S(2)}) async-start(f32[16,1,4608]{2,1,0:T(1,128)} %copy.104), calls=%async_computation.1 | async-start | bytes 589824 | tf_op jit(solution)/shard_map/all_to_all | solution.py:100
  61.7 10.5 %all-to-all-start.3 = ((bf16[2,128,768]{2,1,0:T(8,128)(2,1)}), bf16[2,128,768]{2,1,0:T(8,128)(2,1)S(1)}, u32[]{:S(2)}, u32[]{:S(2)}) async-start(bf16[2,128,768]{2,1,0:T(8,128)(2,1)} %param.16), calls=%async_computation.3 | async-start | bytes 786432 | tf_op jit(solution)/shard_map/all_to_all | solution.py:90
  65.5 365.0 %reduce-scatter.4.cloned.1.call-start = ((), (), s32[]{:S(2)}) async-start(), calls=%async_computation.12 | async-start | bytes 14800896
  212.7 7.0 %copy-start.16 = (bf16[768,3072]{1,0:T(8,128)(2,1)S(1)}, bf16[768,3072]{1,0:T(8,128)(2,1)}, u32[]{:S(2)}) copy-start(bf16[768,3072]{1,0:T(8,128)(2,1)} %all-gather.9.cloned.1.call-done) | copy-start | bytes 14155780
  219.7 1.5 copy-start.17
  219.8 2.4 copy-start.19
  219.8 4.0 copy-start.2
  226.7 2.0 copy-start.3
  228.0 0.8 copy-start.5
  230.2 5.0 %copy-start.12 = (bf16[256,768]{0,1:T(8,128)(2,1)S(1)}, bf16[256,768]{0,1:T(8,128)(2,1)}, u32[]{:S(2)}) copy-start(bf16[256,768]{0,1:T(8,128)(2,1)} %copy.109) | copy-start | bytes 1179652
  235.2 1.9 copy-start.1
  240.5 2.5 copy-start.9
  240.6 2.5 copy-start.20
  243.1 4.6 %copy-start.10 = (bf16[1,1,12,256,64]{3,4,2,1,0:T(8,128)(2,1)S(1)}, bf16[1,1,12,256,64]{3,4,2,1,0:T(8,128)(2,1)}, u32[]{:S(2)}) copy-start(bf16[1,1,12,256,64]{3,4,2,1,0:T(8,128)(2,1)} %fusion.22) | copy-start | bytes 1179652
  255.6 2.5 copy-start.18
  258.0 3.7 copy-start.13
  261.8 2.9 copy-start.6
  261.8 2.9 copy-start.11
  267.0 1.0 copy-start.14
  273.2 10.8 %all-to-all-start.2 = ((bf16[2,2,49152]{2,1,0:T(2,128)(2,1)}), bf16[2,2,49152]{2,1,0:T(2,128)(2,1)S(1)}, u32[]{:S(2)}, u32[]{:S(2)}) async-start(bf16[2,2,49152]{2,1,0:T(2,128)(2,1)} %reshape.781), calls=%async_computation.2 | async-start | bytes 786432 | tf_op jit(solution)/shard_map/all_to_all | solution.py:145
  276.8 4.0 copy-start.7
  276.8 4.0 copy-start.8
  284.0 14.2 %all-to-all-start.4 = ((f32[1,256,768]{2,0,1:T(1,128)}), f32[1,256,768]{2,0,1:T(1,128)S(1)}, u32[]{:S(2)}, u32[]{:S(2)}) async-start(f32[1,256,768]{2,0,1:T(1,128)} %copy.113), calls=%async_computation.4 | async-start | bytes 1572864 | tf_op jit(solution)/shard_map/all_to_all | solution.py:194
  299.4 23.6 %all-to-all-start.5 = ((f32[32,1,4608]{2,1,0:T(1,128)}), f32[32,1,4608]{2,1,0:T(1,128)S(1)}, u32[]{:S(2)}, u32[]{:S(2)}) async-start(f32[32,1,4608]{2,1,0:T(1,128)} %broadcast_in_dim.11), calls=%async_computation.5 | async-start | bytes 1179648 | tf_op jit(solution)/shard_map/all_to_all | solution.py:207
  302.4 34.6 %copy-start.15 = (bf16[2,768]{1,0:T(2,128)(2,1)S(1)}, bf16[2,768]{1,0:T(2,128)(2,1)}, u32[]{:S(2)}) copy-start(bf16[2,768]{1,0:T(2,128)(2,1)} %param.15) | copy-start | bytes 9220
  323.9 11.8 %all-to-all-start.6 = ((f32[16,1,96]{2,1,0:T(1,128)}), f32[16,1,96]{2,1,0:T(1,128)S(1)}, u32[]{:S(2)}, u32[]{:S(2)}) async-start(f32[16,1,96]{2,1,0:T(1,128)} %bitcast.29), calls=%async_computation.6 | async-start | bytes 16384 | tf_op jit(solution)/shard_map/all_to_all | solution.py:262
  430.5 5.0 %copy-start.4 = (bf16[24,9344]{1,0:T(8,128)(2,1)S(1)}, bf16[24,9344]{1,0:T(8,128)(2,1)}, u32[]{:S(2)}) copy-start(bf16[24,9344]{1,0:T(8,128)(2,1)} %reduce-scatter.4.cloned.1.call-done) | copy-start | bytes 1345540
Sparse Core Ops, SparseCore 0:
  10.3 55.0 all-gather.4
  67.7 36.8 all-gather.6
  106.9 51.9 all-gather.10
  161.0 51.6 all-gather.8
  267.1 163.3 reduce-scatter.3
